TPU v7x, 32 devices: a whole 2x2x4 slice. The times are simulated.
32 devices in a mesh: batch: 16 (over z, y, x), stream: 2 (over core).
Axes of the slice: x: 2, y: 2, z: 4, core: 2. Of those that a mesh axis runs over, the one named last changes fastest.
Arguments:
- tokens: bfloat16 [128, 198, 768], P(('batch', 'stream')), may hold values from -6 to 6
- prompts: float32 [50, 768], replicated, may hold values from -6 to 6
- keep_mask: int32 [128, 196], P(('batch', 'stream')), may hold values from 0 to 1, as said below
- counts: int32 [128], P(('batch', 'stream')), may hold values from 79 to 196, as said below
- ln1_gain: float32 [768], replicated, may hold values from 0.5 to 1.5
- ln1_bias: float32 [768], replicated, may hold values from -0.6 to 0.6
- w_qkv: bfloat16 [768, 2304], replicated, may hold values from -0.21875 to 0.21875
- q_bias: float32 [768], replicated, may hold values from -0.6 to 0.6
- v_bias: float32 [768], replicated, may hold values from -0.6 to 0.6
- w_out: bfloat16 [768, 768], replicated, may hold values from -2.5 to 2.5
- out_bias: float32 [768], replicated, may hold values from -0.6 to 0.6
- ln2_gain: float32 [768], replicated, may hold values from 0.5 to 1.5
- ln2_bias: float32 [768], replicated, may hold values from -0.6 to 0.6
- w_fc1: bfloat16 [768, 3072], replicated, may hold values from -0.21875 to 0.21875
- fc1_bias: float32 [3072], replicated, may hold values from -0.6 to 0.6
- w_fc2: bfloat16 [3072, 768], replicated, may hold values from -0.109375 to 0.109375
- fc2_bias: float32 [768], replicated, may hold values from -0.6 to 0.6
- cot_seq: bfloat16 [128, 198, 768], P(('batch', 'stream')), may hold values from -6 to 6
- cot_prompt: bfloat16 [128, 50, 768], P(('batch', 'stream')), may hold values from -6 to 6
Outputs:
- layer_out: bfloat16 [128, 198, 768], P(('batch', 'stream'))
- prompt_out: bfloat16 [128, 50, 768], P(('batch', 'stream'))
- input_grad: float32 [128, 198, 768], P(('batch', 'stream'))
- prompt_grad: float32 [50, 768], replicated
- penalty: float32 [], replicated
Inputs may be any that keep to these rules, and one draw needn't show every extreme that they name: `keep_mask`: 1 keeps a patch; row i has exactly counts[i] ones. counts[i] is the number of ones in row i of keep_mask.
All inputs are finite; a program needn't handle non-finite values.
Results may differ from a plain program's by a relative error of at most 0.01.
Values sent between devices are 32-bit elements; how exact they have to be, the bound alone decides.
A program may use at most 128 MiB of HBM per device.

v0:
```python
import math
import jax
import jax.numpy as jnp
from jax import lax
from jax.sharding import PartitionSpec as P

HEADS = 12
EPSILON = 1e-06


def layer_norm(values_in, norm_gain, norm_shift):
    row_mean = jnp.mean(values_in, axis=-1, keepdims=True)
    centered = values_in - row_mean
    variance = jnp.mean(centered * centered, axis=-1, keepdims=True)
    return centered * lax.rsqrt(variance + EPSILON) * norm_gain + norm_shift


def split_heads(tensor, head_count):
    return tensor.reshape(
        tensor.shape[0], tensor.shape[1], head_count, tensor.shape[2] // head_count
    )


def masked_scores(queries, key_part, live_keys, head_count, score_scale):
    raw_scores = jnp.einsum(
        "iqhd,ikhd->ihqk",
        split_heads(queries, head_count),
        split_heads(key_part, head_count),
        preferred_element_type=jnp.float32,
    )
    return jnp.where(live_keys[:, None, None, :], raw_scores * score_scale, -1e30)


def project_pairs(pair_grads, pair_weight):
    return jnp.einsum("pe,de->pd", pair_grads, pair_weight, precision=lax.Precision.HIGHEST)


def body(
    tokens,
    prompts,
    keep_mask,
    counts,
    ln1_gain,
    ln1_bias,
    w_qkv,
    q_bias,
    v_bias,
    w_out,
    out_bias,
    ln2_gain,
    ln2_bias,
    w_fc1,
    fc1_bias,
    w_fc2,
    fc2_bias,
    cot_seq,
    cot_prompt,
):
    images, seq_length, model_width = tokens.shape
    prompt_count = prompts.shape[0]
    head_count = HEADS
    score_scale = (model_width // head_count) ** (-0.5)
    total_images = images * lax.axis_size("batch") * lax.axis_size("stream")
    count_sum = jnp.sum(counts.astype(jnp.float32))
    kept_total = lax.psum(count_sum, ("batch", "stream"))
    keep_full = jnp.concatenate(
        [jnp.ones((images, seq_length - keep_mask.shape[1]), jnp.int32), keep_mask], axis=1
    )
    kept_cols = keep_full[:, :, None] > 0
    live_keys = (
        jnp.concatenate([jnp.ones((images, prompt_count), jnp.int32), keep_full], axis=1) > 0
    )
    prompt_normed, prompt_norm_back = jax.vjp(
        lambda rows_in: layer_norm(rows_in, ln1_gain, ln1_bias), prompts
    )
    prompt_proj = jnp.dot(
        prompt_normed.astype(jnp.bfloat16), w_qkv, preferred_element_type=jnp.float32
    )
    prompt_query = (prompt_proj[:, :model_width] + q_bias).astype(jnp.bfloat16)
    prompt_pairs = jnp.concatenate(
        [prompt_proj[:, model_width : 2 * model_width], prompt_proj[:, 2 * model_width :] + v_bias],
        axis=1,
    ).astype(jnp.bfloat16)
    token_rows = tokens.astype(jnp.float32)
    token_normed, token_norm_back = jax.vjp(
        lambda rows_in: layer_norm(rows_in, ln1_gain, ln1_bias), token_rows
    )
    token_proj = jnp.einsum(
        "ihd,de->ihe", token_normed.astype(jnp.bfloat16), w_qkv, preferred_element_type=jnp.float32
    )
    token_query = (token_proj[..., :model_width] + q_bias).astype(jnp.bfloat16)
    token_pairs = jnp.concatenate(
        [
            token_proj[..., model_width : 2 * model_width],
            token_proj[..., 2 * model_width :] + v_bias,
        ],
        axis=2,
    ).astype(jnp.bfloat16)
    queries = jnp.concatenate(
        [jnp.broadcast_to(prompt_query[None], (images, prompt_count, model_width)), token_query],
        axis=1,
    )
    pairs = jnp.concatenate(
        [
            jnp.broadcast_to(prompt_pairs[None], (images, prompt_count, 2 * model_width)),
            token_pairs,
        ],
        axis=1,
    )
    key_part = pairs[..., :model_width]
    value_part = pairs[..., model_width:]
    value_heads = split_heads(value_part, head_count)
    scores = masked_scores(queries, key_part, live_keys, head_count, score_scale)
    top_score = jnp.max(scores, axis=-1, keepdims=True)
    log_total = top_score + jnp.log(jnp.sum(jnp.exp(scores - top_score), axis=-1, keepdims=True))
    soft_low = jnp.exp(scores - log_total).astype(jnp.bfloat16)
    context = jnp.einsum(
        "ihqk,ikhd->iqhd", soft_low, value_heads, preferred_element_type=jnp.float32
    )
    context = context.reshape(images, -1, model_width).astype(jnp.bfloat16)
    attention = (
        jnp.einsum("ird,de->ire", context, w_out, preferred_element_type=jnp.float32) + out_bias
    )
    residual = jnp.concatenate(
        [jnp.broadcast_to(prompts[None], (images, prompt_count, model_width)), token_rows], axis=1
    )
    middle = residual + attention
    second_norm, second_norm_back = jax.vjp(
        lambda rows_in: layer_norm(rows_in, ln2_gain, ln2_bias), middle
    )
    hidden = (
        jnp.einsum(
            "ird,df->irf",
            second_norm.astype(jnp.bfloat16),
            w_fc1,
            preferred_element_type=jnp.float32,
        )
        + fc1_bias
    )
    activated, gelu_back = jax.vjp(lambda rows_in: jax.nn.gelu(rows_in, approximate=False), hidden)
    result = (
        middle
        + jnp.einsum(
            "irf,fd->ird", activated.astype(jnp.bfloat16), w_fc2, preferred_element_type=jnp.float32
        )
        + fc2_bias
    )
    prompt_out = result[:, :prompt_count].astype(jnp.bfloat16)
    layer_out = jnp.where(kept_cols, result[:, prompt_count:], token_rows).astype(jnp.bfloat16)
    grad_result = jnp.concatenate(
        [cot_prompt, jnp.where(kept_cols, cot_seq, jnp.zeros_like(cot_seq))], axis=1
    )
    grad_act = jnp.einsum("ird,fd->irf", grad_result, w_fc2, preferred_element_type=jnp.float32)
    grad_hidden = gelu_back(grad_act)[0].astype(jnp.bfloat16)
    grad_second = jnp.einsum("irf,df->ird", grad_hidden, w_fc1, preferred_element_type=jnp.float32)
    grad_middle = grad_result.astype(jnp.float32) + second_norm_back(grad_second)[0]
    grad_context = jnp.einsum(
        "ire,de->ird", grad_middle.astype(jnp.bfloat16), w_out, preferred_element_type=jnp.float32
    ).astype(jnp.bfloat16)
    again = masked_scores(queries, key_part, live_keys, head_count, score_scale)
    soft_full = jnp.exp(again - log_total)
    soft_back = soft_full.astype(jnp.bfloat16)
    context_heads = split_heads(grad_context, head_count)
    grad_soft = jnp.einsum(
        "iqhd,ikhd->ihqk", context_heads, value_heads, preferred_element_type=jnp.float32
    )
    grad_values = jnp.einsum(
        "ihqk,iqhd->ikhd", soft_back, context_heads, preferred_element_type=jnp.float32
    ).reshape(images, -1, model_width)
    row_dot = jnp.sum(soft_full * grad_soft, axis=-1, keepdims=True)
    grad_scores = (soft_full * (grad_soft - row_dot)).astype(jnp.bfloat16)
    grad_queries = (
        jnp.einsum(
            "ihqk,ikhd->iqhd",
            grad_scores,
            split_heads(key_part, head_count),
            preferred_element_type=jnp.float32,
        )
        * score_scale
    )
    grad_queries = grad_queries.reshape(images, -1, model_width).astype(jnp.bfloat16)
    grad_keys = (
        jnp.einsum(
            "ihqk,iqhd->ikhd",
            grad_scores,
            split_heads(queries, head_count),
            preferred_element_type=jnp.float32,
        )
        * score_scale
    ).reshape(images, -1, model_width)
    grad_pairs = jnp.concatenate([grad_keys, grad_values], axis=2)
    token_proj_grad = jnp.concatenate(
        [grad_queries[:, prompt_count:], grad_pairs[:, prompt_count:].astype(jnp.bfloat16)], axis=2
    )
    grad_token_normed = jnp.einsum(
        "ihe,de->ihd", token_proj_grad, w_qkv, preferred_element_type=jnp.float32
    )
    grad_tokens = grad_middle[:, prompt_count:] + token_norm_back(grad_token_normed)[0]
    input_grad = jnp.where(kept_cols, grad_tokens, cot_seq.astype(jnp.float32))
    pair_weight = w_qkv[:, model_width:].astype(jnp.float32)
    pair_local = jnp.sum(grad_pairs[:, :prompt_count], axis=0)
    query_normed = jnp.sum(
        jnp.einsum(
            "ipe,de->ipd",
            grad_queries[:, :prompt_count],
            w_qkv[:, :model_width],
            preferred_element_type=jnp.float32,
        ),
        axis=0,
    )
    middle_sum = jnp.sum(grad_middle[:, :prompt_count], axis=0)
    prompt_local = prompt_norm_back(query_normed)[0] + middle_sum
    pair_total = lax.psum(pair_local, ("batch", "stream"))
    prompt_total = lax.psum(prompt_local, ("batch", "stream"))
    prompt_total = prompt_total + prompt_norm_back(project_pairs(pair_total, pair_weight))[0]
    penalty_weight = kept_total / (keep_mask.shape[1] * math.sqrt(total_images))
    prompt_grad = prompt_total + 2.0 * penalty_weight * prompts
    penalty = penalty_weight * jnp.sum(prompts * prompts) / (prompt_count * model_width)
    return (layer_out, prompt_out, input_grad, prompt_grad, penalty)


def solution(mesh):
    in_specs = (
        P(("batch", "stream"), None, None),
        P(),
        P(("batch", "stream"), None),
        P(("batch", "stream")),
        P(),
        P(),
        P(),
        P(),
        P(),
        P(),
        P(),
        P(),
        P(),
        P(),
        P(),
        P(),
        P(),
        P(("batch", "stream"), None, None),
        P(("batch", "stream"), None, None),
    )
    out_specs = (
        P(("batch", "stream"), None, None),
        P(("batch", "stream"), None, None),
        P(("batch", "stream"), None, None),
        P(),
        P(),
    )
    return jax.shard_map(body, mesh=mesh, in_specs=in_specs, out_specs=out_specs, check_vma=False)
```

profile of v0, /device:TPU:10, one launch (start us, length us, event | category | flops | bytes accessed | tf_op | source)
XLA Modules:
  0.0 464.4 jit_solution(8597299555711745016)
XLA Ops:
  10.7 5.8 %fusion.29 = f32[4,198,2304]{2,1,0:T(8,128)S(1)} fusion(bf16[768,2304]{1,0:T(8,128)(2,1)} %param.25, f32[768]{0:T(1024)} %param.24, f32[768]{0:T(1024)} %param.23, f32[4,198]{1,0:T(4,128)S(1)} %fusion.73, f32[4,198]{1,0:T(4,128)S(1)} %broadcast_multiply_fusion.1, bf16[4,198,768]{2,0,1:T(4,128)(2,1)} %param.19), kind=kOutput, calls=%fused_computation.49 | convolution fusion | flops 2806493184 | bytes 12067008 | tf_op jit(solution)/shard_map/ihd,de->ihe/dot_general | solution.py:88
  16.5 3.0 copy-done.17
  23.8 4.0 fusion.35
  42.9 5.0 %fusion.6 = (f32[4,12,248]{2,1,0:T(8,128)S(1)}, f32[4,12,248,248]{2,3,1,0:T(8,128)S(1)}) fusion(pred[4,248]{1,0:T(4,128)(4,1)S(1)} %add_compare_fusion, bf16[4,248,12,64]{1,3,2,0:T(8,128)(2,1)} %bitcast.72, bf16[4,248,12,64]{1,3,2,0:T(8,128)(2,1)} %bitcast.70), kind=kOutput, calls=%fused_computation.26 | convolution fusion | flops 386725248 | bytes 14904800 | tf_op jit(solution)/shard_map/iqhd,ikhd->ihqk/dot_general | solution.py:25
  47.9 3.4 exponential_reduce_fusion
  52.5 3.1 convolution_convert_fusion
  58.8 13.1 %fusion.32 = (u8[248,3072]{1,0:T(8,128)(4,1)S(1)}, u8[248,3072]{1,0:T(8,128)(4,1)S(1)}, f32[4,248,3072]{2,1,0:T(8,128)}) fusion(f32[3072]{0:T(1024)S(1)} %copy-done.29, bf16[768,3072]{1,0:T(8,128)(2,1)S(1)} %bitcast.83, f32[4,248,768]{2,1,0:T(8,128)S(1)} %get-tuple-element.36, f32[768]{0:T(1024)S(1)} %copy-done.34, f32[768]{0:T(1024)S(1)} %copy-done.25, ...), kind=kOutput, calls=%fused_computation.60 | convolution fusion | flops 4725792768 | bytes 21505792 | tf_op jit(solution)/shard_map/ird,df->irf/dot_general | solution.py:132
  71.9 29.0 %fusion = f32[4,248,3072]{2,1,0:T(8,128)} fusion(f32[4,248,3072]{2,1,0:T(8,128)} %get-tuple-element.37, f32[3072]{0:T(1024)S(1)} %copy-done.29, u8[248,3072]{1,0:T(8,128)(4,1)S(1)} %get-tuple-element.16, u8[248,3072]{1,0:T(8,128)(4,1)S(1)} %get-tuple-element.15), kind=kLoop, calls=%fused_computation.1 | loop fusion | flops 207224832 | bytes 25915392 | tf_op jit(solution)/shard_map/jvp()/erfc | solution.py:140
  100.9 14.7 %add_add_fusion.3 = bf16[4,248,768]{2,1,0:T(8,128)(2,1)S(1)} fusion(f32[4,248,768]{2,1,0:T(8,128)S(1)} %get-tuple-element.36, bf16[3072,768]{1,0:T(8,128)(2,1)} %param.34, f32[4,248,3072]{2,1,0:T(8,128)} %fusion, f32[4,248,3072]{2,1,0:T(8,128)} %get-tuple-element.37, f32[3072]{0:T(1024)S(1)} %copy-done.29, f32[768]{0:T(1024)S(1)} %copy-done.35), kind=kOutput, calls=%fused_computation.56 | convolution fusion | flops 4695318528 | bytes 33684480 | tf_op jit(solution)/shard_map/irf,fd->ird/dot_general | solution.py:143
  117.9 19.5 %multiply_reduce_fusion.1 = (f32[4,248]{1,0:T(4,128)S(1)}, f32[4,248,768]{2,1,0:T(8,128)}) fusion(f32[4,248,768]{2,1,0:T(8,128)} %copy-done.4, f32[768]{0:T(1024)S(1)} %copy-done.25, f32[4,248]{1,0:T(4,128)S(1)} %broadcast_multiply_fusion, bf16[768,3072]{1,0:T(8,128)(2,1)} %param.32, f32[4,248,3072]{2,1,0:T(8,128)} %fusion, ...), kind=kOutput, calls=%fused_computation.55 | convolution fusion | flops 9413491712 | bytes 41458432 | tf_op jit(solution)/shard_map/irf,df->ird/dot_general | solution.py:155
  137.5 3.5 fusion.60
  151.5 14.3 %multiply_reduce_fusion = (f32[4,12,248]{2,1,0:T(8,128)S(1)}, f32[4,12,248,248]{2,3,1,0:T(8,128)}) fusion(f32[4,12,248,248]{2,3,1,0:T(8,128)} %copy-done.1, f32[4,12,248]{2,1,0:T(8,128)S(1)} %log_add_fusion, pred[4,248]{1,0:T(4,128)(4,1)S(1)} %add_compare_fusion, bf16[4,248,12,64]{1,3,2,0:T(8,128)(2,1)} %bitcast.74, bf16[4,248,12,64]{1,3,2,0:T(8,128)(2,1)} %bitcast.80), kind=kOutput, calls=%fused_computation.8 | convolution fusion | flops 392629632 | bytes 26761184 | tf_op jit(solution)/shard_map/iqhd,ikhd->ihqk/dot_general | solution.py:164
  165.8 9.0 %fusion.64 = f32[4,12,64,248]{3,2,1,0:T(8,128)} fusion(bf16[4,248,12,64]{1,3,2,0:T(8,128)(2,1)S(1)} %bitcast.75, f32[4,12,248,248]{2,3,1,0:T(8,128)} %copy-done.1, f32[4,12,248]{2,1,0:T(8,128)S(1)} %log_add_fusion, pred[4,248]{1,0:T(4,128)(4,1)S(1)} %add_compare_fusion), kind=kOutput, calls=%fused_computation.121 | convolution fusion | flops 389689344 | bytes 16428512 | tf_op jit(solution)/shard_map/ihqk,iqhd->ikhd/dot_general | solution.py:167
  174.8 6.9 %multiply_convert_fusion = bf16[4,12,248,248]{2,3,1,0:T(8,128)(2,1)S(1)} fusion(f32[4,12,248,248]{2,3,1,0:T(8,128)} %get-tuple-element.41, f32[4,12,248,248]{2,3,1,0:T(8,128)S(1)} %bitcast.69, f32[4,12,248]{2,1,0:T(8,128)S(1)} %get-tuple-element.40, f32[4,12,248]{2,1,0:T(8,128)S(1)} %log_add_fusion, pred[4,248]{1,0:T(4,128)(4,1)S(1)} %add_compare_fusion), kind=kLoop, calls=%fused_computation.7 | loop fusion | flops 17713152 | bytes 29618144 | tf_op jit(solution)/shard_map/convert_element_type | solution.py:171
  181.8 3.7 convolution_multiply_fusion
  185.5 3.5 copy.61
  189.0 3.6 copy.62
  195.1 4.5 fusion.13
  199.6 4.0 multiply_convert_fusion.3
  209.0 6.3 %multiply_reduce_fusion.3 = (f32[4,198]{1,0:T(4,128)S(1)}, f32[4,198,768]{2,1,0:T(8,128)S(1)}) fusion(f32[768]{0:T(1024)S(1)} %copy-done.24, f32[4,198]{1,0:T(4,128)S(1)} %broadcast_multiply_fusion.1, bf16[4,198,768]{2,0,1:T(4,128)(2,1)S(1)} %copy-done.3, bf16[768,2304]{1,0:T(8,128)(2,1)} %param.25, bf16[4,198,1536]{2,1,0:T(8,128)(2,1)} %fusion.13, ...), kind=kOutput, calls=%fused_computation.70 | convolution fusion | flops 2813183232 | bytes 10847424 | tf_op jit(solution)/shard_map/ihe,de->ihd/dot_general | solution.py:195
  222.3 41.6 %psum.23 = f32[]{:T(128)} all-reduce(f32[]{:T(128)} %convert_reduce_fusion.1), channel_id=1, replica_groups=mesh['batch'=16,'stream'=2] {'batch','stream'}, use_global_device_ids=true, to_apply=%region_23.24 | all-reduce | flops 1 | bytes 8 | tf_op jit(solution)/shard_map/psum | solution.py:65
  272.5 51.0 %all-reduce.6.cloned.1.call-done = f32[50,1536]{1,0:T(8,128)} async-done(((f32[50,1536]{1,0:T(8,128)}), f32[50,1536]{1,0:T(8,128)}) %all-reduce.6.cloned.1.call-update) | async-done | bytes 307216 | tf_op jit(solution)/shard_map/psum | solution.py:213
  323.6 4.6 multiply_reduce_fusion.5
  330.0 124.4 %all-reduce.4.cloned.1.call-done = f32[50,768]{1,0:T(8,128)} async-done(((f32[50,768]{1,0:T(8,128)}), f32[50,768]{1,0:T(8,128)}) %all-reduce.4.cloned.1.call-update) | async-done | bytes 153616 | tf_op jit(solution)/shard_map/psum | solution.py:214
  (152 shorter events, 64.9 us)
Async XLA Ops:
  7.2 48.5 %copy-start = (bf16[768,768]{1,0:T(8,128)(2,1)S(1)}, bf16[768,768]{1,0:T(8,128)(2,1)}, u32[]{:S(2)}) copy-start(bf16[768,768]{1,0:T(8,128)(2,1)} %param.28) | copy-start | bytes 3538948
  7.2 316.4 %all-reduce.6.cloned.1.call-start = ((), (), s32[]{:S(2)}) async-start(), calls=%async_computation.1 | async-start | bytes 688128 | tf_op jit(solution)/shard_map/psum | solution.py:213
  10.6 10.0 %copy-start.12 = (f32[50,768]{1,0:T(8,128)S(1)}, f32[50,768]{1,0:T(8,128)}, u32[]{:S(2)}) copy-start(f32[50,768]{1,0:T(8,128)} %param.20) | copy-start | bytes 460804
  10.6 10.3 %copy-start.24 = (f32[768]{0:T(1024)S(1)}, f32[768]{0:T(1024)}, u32[]{:S(2)}) copy-start(f32[768]{0:T(1024)} %param.23) | copy-start | bytes 9220
  10.7 10.3 %copy-start.30 = (f32[768]{0:T(1024)S(1)}, f32[768]{0:T(1024)}, u32[]{:S(2)}) copy-start(f32[768]{0:T(1024)} %param.24) | copy-start | bytes 9220
  19.5 4.3 copy-start.26
  19.5 4.3 copy-start.27
  23.8 4.1 copy-start.3
  47.9 4.6 copy-start.1
  47.9 4.6 copy-start.16
  57.5 43.4 %copy-start.4 = (f32[4,248,768]{2,1,0:T(8,128)}, f32[4,248,768]{2,1,0:T(8,128)S(1)}, u32[]{:S(2)}) copy-start(f32[4,248,768]{2,1,0:T(8,128)S(1)} %get-tuple-element.36) | copy-start | bytes 9142276
  71.9 29.0 %copy-start.35 = (f32[768]{0:T(1024)S(1)}, f32[768]{0:T(1024)}, u32[]{:S(2)}) copy-start(f32[768]{0:T(1024)} %param.35) | copy-start | bytes 9220
  100.9 14.7 %copy-start.19 = (bf16[4,198,768]{2,0,1:T(4,128)(2,1)S(1)}, bf16[4,198,768]{2,0,1:T(4,128)(2,1)}, u32[]{:S(2)}) copy-start(bf16[4,198,768]{2,0,1:T(4,128)(2,1)} %param.36) | copy-start | bytes 3649540
  137.5 4.6 copy-start.11
  151.5 14.4 %copy-start.8 = (bf16[4,248,768]{1,2,0:T(8,128)(2,1)S(1)}, bf16[4,248,768]{1,2,0:T(8,128)(2,1)}, u32[]{:S(2)}) copy-start(bf16[4,248,768]{1,2,0:T(8,128)(2,1)} %copy.56) | copy-start | bytes 4571140
  151.5 23.4 %slice-start = ((s8[12189696]{0:T(1024)(128)(4,1)}), s8[4194304]{0:T(1024)(128)(4,1)S(1)}, s32[]{:S(2)}) async-start(s8[12189696]{0:T(1024)(128)(4,1)} %bitcast.68), calls=%async_computation.2 | async-start | bytes 8388608
  151.5 23.4 %slice-start.1 = ((s8[12189696]{0:T(1024)(128)(4,1)}), s8[3801088]{0:T(1024)(128)(4,1)S(1)}, s32[]{:S(2)}) async-start(s8[12189696]{0:T(1024)(128)(4,1)} %bitcast.68), calls=%async_computation.3 | async-start | bytes 7602176
  165.8 9.0 %slice-start.2 = ((s8[12189696]{0:T(1024)(128)(4,1)}), s8[4194304]{0:T(1024)(128)(4,1)S(1)}, s32[]{:S(2)}) async-start(s8[12189696]{0:T(1024)(128)(4,1)} %bitcast.68), calls=%async_computation.4 | async-start | bytes 8388608
  174.8 7.0 %copy-start.7 = (bf16[4,248,768]{1,2,0:T(8,128)(2,1)S(1)}, bf16[4,248,768]{1,2,0:T(8,128)(2,1)}, u32[]{:S(2)}) copy-start(bf16[4,248,768]{1,2,0:T(8,128)(2,1)} %copy.50) | copy-start | bytes 4571140
  194.8 259.7 %all-reduce.4.cloned.1.call-start = ((), (), s32[]{:S(2)}) async-start(), calls=%async_computation | async-start | bytes 344064 | tf_op jit(solution)/shard_map/psum | solution.py:214
  195.1 4.6 copy-start.6
  209.0 7.3 %copy-start.20 = (bf16[4,198,768]{2,0,1:T(4,128)(2,1)S(1)}, bf16[4,198,768]{2,0,1:T(4,128)(2,1)}, u32[]{:S(2)}) copy-start(bf16[4,198,768]{2,0,1:T(4,128)(2,1)} %param.36) | copy-start | bytes 3649540
  220.2 46.6 %slice-start.3 = ((bf16[4,248,768]{2,1,0:T(8,128)(2,1)}), bf16[4,50,768]{2,1,0:T(8,128)(2,1)S(1)}, s32[]{:S(2)}) async-start(bf16[4,248,768]{2,1,0:T(8,128)(2,1)} %copy-done.22), calls=%async_computation.5 | async-start | bytes 688128 | tf_op jit(solution)/shard_map/slice | solution.py:148
  270.1 58.1 %copy-start.32 = (f32[50]{0:T(128)S(1)}, f32[50]{0:T(128)}, u32[]{:S(2)}) copy-start(f32[50]{0:T(128)} %copy-done.31) | copy-start | bytes 604
  (21 other events, 50.5 us)
Sparse Core Ops, SparseCore 0:
  194.9 128.5 all-reduce.5
  330.6 123.8 all-reduce.3
where the time goes:
time: 470 us; the launch traced here: 464 us
  waiting for transfers between devices  175 us (37%)
  matrix products  112 us (24%)
  other arithmetic  75.7 us (16%)
  blocking collectives  41.6 us (9%)
  local copies, waits for them, and re-layouts  41.1 us (9%)
  between operations  17.9 us (4%)
    psum x1, waiting for transfers between devices, body(): prompt_total = lax.psum(prompt_local, ('batch', 'stream'))  124 us
    psum x1, waiting for transfers between devices, body(): pair_total = lax.psum(pair_local, ('batch', 'stream'))  51 us
    psum x1, blocking collectives, body(): kept_total = lax.psum(count_sum, ('batch', 'stream'))  41.6 us
    another operation x1, other arithmetic, body(): jax.nn.gelu(rows_in, approximate=False)  29 us
    dot_general x1, matrix products, body(): jnp.einsum('irf,df->ird', grad_hidden, w_fc1, preferred_element_type=jnp....  19.5 us
    unnamed x89, local copies, waits for them, and re-layouts  18.5 us
    dot_general x1, matrix products, body(): jnp.einsum('irf,fd->ird', activated.astype(jnp.bfloat16), w_fc2, preferre...  14.7 us
    dot_general x1, matrix products, body(): jnp.einsum('iqhd,ikhd->ihqk', context_heads, value_heads, preferred_eleme...  14.3 us
  transfers between devices with their start and end apart: 2, of which 2 were waited for; matrix products, arithmetic and copies ran while one was open for 7% of the time, Pallas kernels for 0%

commit v1 on v0

--- a/solution.py
+++ b/solution.py
@@ -210,7 +210,8 @@
     )
     middle_sum = jnp.sum(grad_middle[:, :prompt_count], axis=0)
     prompt_local = prompt_norm_back(query_normed)[0] + middle_sum
-    pair_total = lax.psum(pair_local, ("batch", "stream"))
+    inner = lax.psum(pair_local, "stream")
+    pair_total = lax.psum(inner, "batch")
     prompt_total = lax.psum(prompt_local, ("batch", "stream"))
     prompt_total = prompt_total + prompt_norm_back(project_pairs(pair_total, pair_weight))[0]
     penalty_weight = kept_total / (keep_mask.shape[1] * math.sqrt(total_images))

time: 470 us -> 475 us (1.011)
  waiting for transfers between devices: 175 us -> 181 us
    psum x1 -> x2, waiting for transfers between devices: 51 us -> 55.8 us  [the longest x1 55.8 us: body(): pair_total = lax.psum(inner, 'batch')]
    unnamed x89 -> x87, local copies, waits for them, and re-layouts: 18.5 us -> 18.5 us
  transfers between devices with their start and end apart: 2 -> 3, of which waited for: 2 -> 2; matrix products, arithmetic and copies ran while one was open for 7% -> 7% of each run, Pallas kernels for 0% -> 0%
where the time goes in v1:
time: 475 us; the launch traced here: 470 us
  waiting for transfers between devices  181 us (38%)
  matrix products  113 us (24%)
  other arithmetic  75.7 us (16%)
  blocking collectives  41.7 us (9%)
  local copies, waits for them, and re-layouts  41 us (9%)
  between operations  17.7 us (4%)
    psum x1, waiting for transfers between devices, body(): prompt_total = lax.psum(prompt_local, ('batch', 'stream'))  125 us
    psum x1, waiting for transfers between devices, body(): pair_total = lax.psum(inner, 'batch')  55.8 us
    psum x1, blocking collectives, body(): kept_total = lax.psum(count_sum, ('batch', 'stream'))  41.7 us
    another operation x1, other arithmetic, body(): jax.nn.gelu(rows_in, approximate=False)  29 us
    dot_general x1, matrix products, body(): jnp.einsum('irf,df->ird', grad_hidden, w_fc1, preferred_element_type=jnp....  19.5 us
    unnamed x87, local copies, waits for them, and re-layouts  18.5 us
    dot_general x1, matrix products, body(): jnp.einsum('irf,fd->ird', activated.astype(jnp.bfloat16), w_fc2, preferre...  14.7 us
    dot_general x1, matrix products, body(): jnp.einsum('iqhd,ikhd->ihqk', context_heads, value_heads, preferred_eleme...  14.3 us
  transfers between devices with their start and end apart: 3, of which 2 were waited for; matrix products, arithmetic and copies ran while one was open for 7% of the time, Pallas kernels for 0%

profile of v1, /device:TPU:10, one launch (start us, length us, event | category | flops | bytes accessed | tf_op | source)
XLA Modules:
  0.0 469.9 jit_solution(3961500707316778298)
XLA Ops:
  10.7 5.8 %fusion.29 = f32[4,198,2304]{2,1,0:T(8,128)S(1)} fusion(bf16[768,2304]{1,0:T(8,128)(2,1)} %param.25, f32[768]{0:T(1024)} %param.24, f32[768]{0:T(1024)} %param.23, f32[4,198]{1,0:T(4,128)S(1)} %fusion.73, f32[4,198]{1,0:T(4,128)S(1)} %broadcast_multiply_fusion.1, bf16[4,198,768]{2,0,1:T(4,128)(2,1)} %param.19), kind=kOutput, calls=%fused_computation.49 | convolution fusion | flops 2806493184 | bytes 12067008 | tf_op jit(solution)/shard_map/ihd,de->ihe/dot_general | solution.py:88
  16.5 3.0 copy-done.16
  23.8 4.0 fusion.35
  42.9 5.0 %fusion.6 = (f32[4,12,248]{2,1,0:T(8,128)S(1)}, f32[4,12,248,248]{2,3,1,0:T(8,128)S(1)}) fusion(pred[4,248]{1,0:T(4,128)(4,1)S(1)} %add_compare_fusion, bf16[4,248,12,64]{1,3,2,0:T(8,128)(2,1)} %bitcast.72, bf16[4,248,12,64]{1,3,2,0:T(8,128)(2,1)} %bitcast.70), kind=kOutput, calls=%fused_computation.26 | convolution fusion | flops 386725248 | bytes 14904800 | tf_op jit(solution)/shard_map/iqhd,ikhd->ihqk/dot_general | solution.py:25
  47.9 3.4 exponential_reduce_fusion
  52.5 3.1 convolution_convert_fusion
  58.8 13.1 %fusion.32 = (u8[248,3072]{1,0:T(8,128)(4,1)S(1)}, u8[248,3072]{1,0:T(8,128)(4,1)S(1)}, f32[4,248,3072]{2,1,0:T(8,128)}) fusion(f32[3072]{0:T(1024)S(1)} %copy-done.28, bf16[768,3072]{1,0:T(8,128)(2,1)S(1)} %bitcast.83, f32[4,248,768]{2,1,0:T(8,128)S(1)} %get-tuple-element.36, f32[768]{0:T(1024)S(1)} %copy-done.33, f32[768]{0:T(1024)S(1)} %copy-done.24, ...), kind=kOutput, calls=%fused_computation.60 | convolution fusion | flops 4725792768 | bytes 21505792 | tf_op jit(solution)/shard_map/ird,df->irf/dot_general | solution.py:132
  71.9 29.0 %fusion = f32[4,248,3072]{2,1,0:T(8,128)} fusion(f32[4,248,3072]{2,1,0:T(8,128)} %get-tuple-element.37, f32[3072]{0:T(1024)S(1)} %copy-done.28, u8[248,3072]{1,0:T(8,128)(4,1)S(1)} %get-tuple-element.16, u8[248,3072]{1,0:T(8,128)(4,1)S(1)} %get-tuple-element.15), kind=kLoop, calls=%fused_computation.1 | loop fusion | flops 207224832 | bytes 25915392 | tf_op jit(solution)/shard_map/jvp()/erfc | solution.py:140
  100.9 14.7 %add_add_fusion.3 = bf16[4,248,768]{2,1,0:T(8,128)(2,1)S(1)} fusion(f32[4,248,768]{2,1,0:T(8,128)S(1)} %get-tuple-element.36, bf16[3072,768]{1,0:T(8,128)(2,1)} %param.34, f32[4,248,3072]{2,1,0:T(8,128)} %fusion, f32[4,248,3072]{2,1,0:T(8,128)} %get-tuple-element.37, f32[3072]{0:T(1024)S(1)} %copy-done.28, f32[768]{0:T(1024)S(1)} %copy-done.34), kind=kOutput, calls=%fused_computation.56 | convolution fusion | flops 4695318528 | bytes 33684480 | tf_op jit(solution)/shard_map/irf,fd->ird/dot_general | solution.py:143
  117.9 19.5 %multiply_reduce_fusion.1 = (f32[4,248]{1,0:T(4,128)S(1)}, f32[4,248,768]{2,1,0:T(8,128)}) fusion(f32[4,248,768]{2,1,0:T(8,128)} %copy-done.4, f32[768]{0:T(1024)S(1)} %copy-done.24, f32[4,248]{1,0:T(4,128)S(1)} %broadcast_multiply_fusion, bf16[768,3072]{1,0:T(8,128)(2,1)} %param.32, f32[4,248,3072]{2,1,0:T(8,128)} %fusion, ...), kind=kOutput, calls=%fused_computation.55 | convolution fusion | flops 9413491712 | bytes 41458432 | tf_op jit(solution)/shard_map/irf,df->ird/dot_general | solution.py:155
  137.5 3.5 fusion.60
  151.5 14.3 %multiply_reduce_fusion = (f32[4,12,248]{2,1,0:T(8,128)S(1)}, f32[4,12,248,248]{2,3,1,0:T(8,128)}) fusion(f32[4,12,248,248]{2,3,1,0:T(8,128)} %copy-done.1, f32[4,12,248]{2,1,0:T(8,128)S(1)} %log_add_fusion, pred[4,248]{1,0:T(4,128)(4,1)S(1)} %add_compare_fusion, bf16[4,248,12,64]{1,3,2,0:T(8,128)(2,1)} %bitcast.74, bf16[4,248,12,64]{1,3,2,0:T(8,128)(2,1)} %bitcast.80), kind=kOutput, calls=%fused_computation.8 | convolution fusion | flops 392629632 | bytes 26761184 | tf_op jit(solution)/shard_map/iqhd,ikhd->ihqk/dot_general | solution.py:164
  165.8 9.0 %fusion.64 = f32[4,12,64,248]{3,2,1,0:T(8,128)} fusion(bf16[4,248,12,64]{1,3,2,0:T(8,128)(2,1)S(1)} %bitcast.75, f32[4,12,248,248]{2,3,1,0:T(8,128)} %copy-done.1, f32[4,12,248]{2,1,0:T(8,128)S(1)} %log_add_fusion, pred[4,248]{1,0:T(4,128)(4,1)S(1)} %add_compare_fusion), kind=kOutput, calls=%fused_computation.121 | convolution fusion | flops 389689344 | bytes 16428512 | tf_op jit(solution)/shard_map/ihqk,iqhd->ikhd/dot_general | solution.py:167
  174.8 6.9 %multiply_convert_fusion = bf16[4,12,248,248]{2,3,1,0:T(8,128)(2,1)S(1)} fusion(f32[4,12,248,248]{2,3,1,0:T(8,128)} %get-tuple-element.41, f32[4,12,248,248]{2,3,1,0:T(8,128)S(1)} %bitcast.69, f32[4,12,248]{2,1,0:T(8,128)S(1)} %get-tuple-element.40, f32[4,12,248]{2,1,0:T(8,128)S(1)} %log_add_fusion, pred[4,248]{1,0:T(4,128)(4,1)S(1)} %add_compare_fusion), kind=kLoop, calls=%fused_computation.7 | loop fusion | flops 17713152 | bytes 29618144 | tf_op jit(solution)/shard_map/convert_element_type | solution.py:171
  181.8 3.7 convolution_multiply_fusion
  185.5 3.5 copy.61
  189.0 3.6 copy.62
  195.1 4.5 fusion.13
  199.6 3.9 multiply_convert_fusion.3
  209.0 6.3 %multiply_reduce_fusion.3 = (f32[4,198]{1,0:T(4,128)S(1)}, f32[4,198,768]{2,1,0:T(8,128)S(1)}) fusion(f32[768]{0:T(1024)S(1)} %copy-done.23, f32[4,198]{1,0:T(4,128)S(1)} %broadcast_multiply_fusion.1, bf16[4,198,768]{2,0,1:T(4,128)(2,1)S(1)} %copy-done.3, bf16[768,2304]{1,0:T(8,128)(2,1)} %param.25, bf16[4,198,1536]{2,1,0:T(8,128)(2,1)} %fusion.13, ...), kind=kOutput, calls=%fused_computation.70 | convolution fusion | flops 2813183232 | bytes 10847424 | tf_op jit(solution)/shard_map/ihe,de->ihd/dot_general | solution.py:195
  221.4 41.7 %psum.31 = f32[]{:T(128)} all-reduce(f32[]{:T(128)} %convert_reduce_fusion.1), channel_id=1, replica_groups=mesh['batch'=16,'stream'=2] {'batch','stream'}, use_global_device_ids=true, to_apply=%region_24.25 | all-reduce | flops 1 | bytes 8 | tf_op jit(solution)/shard_map/psum | solution.py:65
  272.9 55.8 %all-reduce.9.cloned.1.call-done = f32[50,1536]{1,0:T(8,128)} async-done(((f32[50,1536]{1,0:T(8,128)}), f32[50,1536]{1,0:T(8,128)}) %all-reduce.9.cloned.1.call-update) | async-done | bytes 307216 | tf_op jit(solution)/shard_map/psum | solution.py:214
  328.7 4.6 multiply_reduce_fusion.5
  335.2 125.1 %all-reduce.5.cloned.1.call-done = f32[50,768]{1,0:T(8,128)} async-done(((f32[50,768]{1,0:T(8,128)}), f32[50,768]{1,0:T(8,128)}) %all-reduce.5.cloned.1.call-update) | async-done | bytes 153616 | tf_op jit(solution)/shard_map/psum | solution.py:215
  (153 shorter events, 65.1 us)
Async XLA Ops:
  7.2 48.5 %copy-start = (bf16[768,768]{1,0:T(8,128)(2,1)S(1)}, bf16[768,768]{1,0:T(8,128)(2,1)}, u32[]{:S(2)}) copy-start(bf16[768,768]{1,0:T(8,128)(2,1)} %param.28) | copy-start | bytes 3538948
  7.2 213.0 %all-reduce.7.cloned.1.call-start = ((), (), s32[]{:S(2)}) async-start(), calls=%async_computation.1 | async-start | bytes 688128 | tf_op jit(solution)/shard_map/psum | solution.py:213
  10.6 10.0 %copy-start.12 = (f32[50,768]{1,0:T(8,128)S(1)}, f32[50,768]{1,0:T(8,128)}, u32[]{:S(2)}) copy-start(f32[50,768]{1,0:T(8,128)} %param.20) | copy-start | bytes 460804
  10.6 10.3 %copy-start.23 = (f32[768]{0:T(1024)S(1)}, f32[768]{0:T(1024)}, u32[]{:S(2)}) copy-start(f32[768]{0:T(1024)} %param.23) | copy-start | bytes 9220
  10.7 10.3 %copy-start.29 = (f32[768]{0:T(1024)S(1)}, f32[768]{0:T(1024)}, u32[]{:S(2)}) copy-start(f32[768]{0:T(1024)} %param.24) | copy-start | bytes 9220
  19.4 4.3 copy-start.25
  19.5 4.3 copy-start.26
  47.9 4.6 copy-start.1
  47.9 4.6 copy-start.15
  57.5 43.4 %copy-start.4 = (f32[4,248,768]{2,1,0:T(8,128)}, f32[4,248,768]{2,1,0:T(8,128)S(1)}, u32[]{:S(2)}) copy-start(f32[4,248,768]{2,1,0:T(8,128)S(1)} %get-tuple-element.36) | copy-start | bytes 9142276
  71.9 29.0 %copy-start.34 = (f32[768]{0:T(1024)S(1)}, f32[768]{0:T(1024)}, u32[]{:S(2)}) copy-start(f32[768]{0:T(1024)} %param.35) | copy-start | bytes 9220
  100.9 14.7 %copy-start.18 = (bf16[4,198,768]{2,0,1:T(4,128)(2,1)S(1)}, bf16[4,198,768]{2,0,1:T(4,128)(2,1)}, u32[]{:S(2)}) copy-start(bf16[4,198,768]{2,0,1:T(4,128)(2,1)} %param.36) | copy-start | bytes 3649540
  137.5 4.6 copy-start.11
  151.5 14.4 %copy-start.8 = (bf16[4,248,768]{1,2,0:T(8,128)(2,1)S(1)}, bf16[4,248,768]{1,2,0:T(8,128)(2,1)}, u32[]{:S(2)}) copy-start(bf16[4,248,768]{1,2,0:T(8,128)(2,1)} %copy.56) | copy-start | bytes 4571140
  151.5 23.4 %slice-start = ((s8[12189696]{0:T(1024)(128)(4,1)}), s8[4194304]{0:T(1024)(128)(4,1)S(1)}, s32[]{:S(2)}) async-start(s8[12189696]{0:T(1024)(128)(4,1)} %bitcast.68), calls=%async_computation.3 | async-start | bytes 8388608
  151.5 23.4 %slice-start.1 = ((s8[12189696]{0:T(1024)(128)(4,1)}), s8[3801088]{0:T(1024)(128)(4,1)S(1)}, s32[]{:S(2)}) async-start(s8[12189696]{0:T(1024)(128)(4,1)} %bitcast.68), calls=%async_computation.4 | async-start | bytes 7602176
  165.8 9.0 %slice-start.2 = ((s8[12189696]{0:T(1024)(128)(4,1)}), s8[4194304]{0:T(1024)(128)(4,1)S(1)}, s32[]{:S(2)}) async-start(s8[12189696]{0:T(1024)(128)(4,1)} %bitcast.68), calls=%async_computation.5 | async-start | bytes 8388608
  174.8 7.0 %copy-start.7 = (bf16[4,248,768]{1,2,0:T(8,128)(2,1)S(1)}, bf16[4,248,768]{1,2,0:T(8,128)(2,1)}, u32[]{:S(2)}) copy-start(bf16[4,248,768]{1,2,0:T(8,128)(2,1)} %copy.50) | copy-start | bytes 4571140
  194.8 133.9 %all-reduce.9.cloned.1.call-start = ((), (), s32[]{:S(2)}) async-start(), calls=%async_computation.2 | async-start | bytes 688128 | tf_op jit(solution)/shard_map/psum | solution.py:214
  195.0 4.6 copy-start.6
  209.0 7.4 %copy-start.19 = (bf16[4,198,768]{2,0,1:T(4,128)(2,1)S(1)}, bf16[4,198,768]{2,0,1:T(4,128)(2,1)}, u32[]{:S(2)}) copy-start(bf16[4,198,768]{2,0,1:T(4,128)(2,1)} %param.36) | copy-start | bytes 3649540
  219.6 46.4 %slice-start.3 = ((bf16[4,248,768]{2,1,0:T(8,128)(2,1)}), bf16[4,50,768]{2,1,0:T(8,128)(2,1)S(1)}, s32[]{:S(2)}) async-start(bf16[4,248,768]{2,1,0:T(8,128)(2,1)} %copy-done.21), calls=%async_computation.6 | async-start | bytes 688128 | tf_op jit(solution)/shard_map/slice | solution.py:148
  220.2 240.0 %all-reduce.5.cloned.1.call-start = ((), (), s32[]{:S(2)}) async-start(), calls=%async_computation | async-start | bytes 344064 | tf_op jit(solution)/shard_map/psum | solution.py:215
  269.2 64.0 %copy-start.31 = (f32[50]{0:T(128)S(1)}, f32[50]{0:T(128)}, u32[]{:S(2)}) copy-start(f32[50]{0:T(128)} %copy-done.30) | copy-start | bytes 604
  (21 other events, 51.5 us)
Sparse Core Ops, SparseCore 0:
  194.9 19.7 all-reduce.6
  220.3 108.2 all-reduce.8
  335.7 124.5 all-reduce.4
